TPU v7x, 128 devices: a whole 4x4x4 slice. The times are simulated.
128 devices in a mesh: grp: 4 (over x), seq: 32 (over y, z, core).
Axes of the slice: x: 4, y: 4, z: 4, core: 2. Of those that a mesh axis runs over, the one named last changes fastest.
Arguments:
- grad_output: bfloat16 [4096, 8192], P('seq', 'grp'), may hold values from -6 to 6
- hidden: bfloat16 [4096, 28672], P('seq', 'grp'), may hold values from -6 to 6
- down_weight: bfloat16 [28672, 8192], P('seq', 'grp'), may hold values from -0.0625 to 0.0625
- adapter_down: bfloat16 [64, 64, 28672], P(None, None, ('grp', 'seq')), may hold values from -0.03125 to 0.03125
- adapter_up: bfloat16 [64, 64, 8192], P(None, None, ('grp', 'seq')), may hold values from -0.0625 to 0.0625
- job_tenant: int32 [32, 4], replicated, may hold values from 0 to 63, all different within a row
- job_count: int32 [32, 4], replicated, may hold values from 1 to 64, 128 in all within a row
Outputs:
- grad_hidden: bfloat16 [4096, 28672], P('seq', 'grp')
- grad_adapter_down: float32 [64, 64, 28672], P(None, None, ('grp', 'seq'))
- grad_adapter_up: float32 [64, 64, 8192], P(None, None, ('grp', 'seq'))
Inputs may be any that keep to these rules, and one draw needn't show every extreme that they name: `job_tenant`: each row names 4 different tenants; every tenant is named by some row. `job_count`: each row sums to 128, and its largest entry is exactly 64.
All inputs are finite; a program needn't handle non-finite values.
Results may differ from a plain program's by a relative error of at most 0.015.
Values may be sent and summed in bfloat16 or wider, within the bound.
A program may use at most 128 MiB of HBM per device.

v0:
```python
import jax
import jax.numpy as jnp
from jax import lax
from jax.sharding import PartitionSpec as P

ADAPTER_SCALE = 2.0


def shards(grad_output, hidden, down_weight, adapter_down, adapter_up, job_tenant, job_count):
    shard_index = lax.axis_index(SEQ)
    shard_count = lax.axis_size(SEQ)
    group_count = lax.axis_size("grp")
    tok_rows = grad_output.shape[0]
    job_slots = job_tenant.shape[1]
    ranks = adapter_down.shape[1]
    down_slab = adapter_down.shape[2]
    up_slab = adapter_up.shape[2]
    tenant_total = adapter_down.shape[0]
    contract_last = (((1,), (1,)), ((), ()))
    contract_rows = (((0,), (0,)), ((), ()))
    tenant_table = (
        job_tenant[:, :, None] == lax.broadcasted_iota(jnp.int32, (1, 1, tenant_total), 2)
    ).astype(jnp.float32)
    totals = jnp.sum(job_count.astype(jnp.float32)[:, :, None] * tenant_table, axis=(0, 1))
    weights = ADAPTER_SCALE / totals
    table_here = lax.dynamic_index_in_dim(tenant_table, shard_index, 0, keepdims=False)
    job_weights = jnp.sum(table_here * weights[None, :], axis=1)
    counts_here = lax.dynamic_index_in_dim(job_count, shard_index, 0, keepdims=False)
    run_ends = jnp.cumsum(counts_here)
    run_starts = run_ends - counts_here
    positions = lax.broadcasted_iota(jnp.int32, (tok_rows, job_slots), 0)
    member = ((positions >= run_starts[None, :]) & (positions < run_ends[None, :])).astype(
        jnp.float32
    )
    chosen = job_tenant.T
    fetched_down, fetched_up = (
        lax.all_to_all(adapter_down[chosen], SEQ, split_axis=1, concat_axis=3, tiled=True),
        lax.all_to_all(adapter_up[chosen], SEQ, split_axis=1, concat_axis=3, tiled=True),
    )
    down_stack = fetched_down.reshape(job_slots * ranks, shard_count * down_slab)
    up_stack = fetched_up.reshape(job_slots * ranks, shard_count * up_slab)

    def select_jobs(projected):
        return jnp.sum(projected.reshape(tok_rows, job_slots, ranks) * member[:, :, None], axis=1)

    grad_proj = lax.dot_general(
        grad_output, up_stack, contract_last, preferred_element_type=jnp.float32
    )
    act_proj = lax.dot_general(
        hidden, down_stack, contract_last, preferred_element_type=jnp.float32
    )
    rank_part = jnp.concatenate([select_jobs(grad_proj), select_jobs(act_proj)], axis=1).astype(
        jnp.bfloat16
    )
    weight_pair = lax.all_gather(down_weight, "core", axis=0, tiled=True)
    tokens_same_core = lax.all_gather(grad_output, "chip", axis=0, tiled=True)
    partial_value = lax.dot_general(
        tokens_same_core, weight_pair, contract_last, preferred_element_type=jnp.float32
    )
    routed = lax.all_to_all(
        partial_value.astype(jnp.bfloat16), "chip", split_axis=0, concat_axis=1, tiled=True
    )
    width_here = routed.shape[1] // group_count
    base_grad = lax.psum_scatter(
        routed.reshape(tok_rows, group_count, width_here), "grp", scatter_dimension=1, tiled=True
    ).reshape(tok_rows, width_here)
    rank_sum = lax.psum(rank_part.astype(jnp.float32), "grp")
    grad_rank = rank_sum[:, :ranks].astype(jnp.bfloat16)
    act_rank = rank_sum[:, ranks:].astype(jnp.bfloat16)
    grad_spread = (
        (member[:, :, None] * lax.optimization_barrier(grad_rank).astype(jnp.float32)[:, None, :])
        .reshape(tok_rows, job_slots * ranks)
        .astype(jnp.bfloat16)
    )
    act_spread = (
        (member[:, :, None] * lax.optimization_barrier(act_rank).astype(jnp.float32)[:, None, :])
        .reshape(tok_rows, job_slots * ranks)
        .astype(jnp.bfloat16)
    )
    adapter_term = (
        jnp.dot(grad_spread, down_stack, preferred_element_type=jnp.float32) * ADAPTER_SCALE
    )
    grad_hidden = (base_grad.astype(jnp.float32) + adapter_term).astype(jnp.bfloat16)
    down_rows = lax.dot_general(
        grad_spread, hidden, contract_rows, preferred_element_type=jnp.float32
    )
    down_rows = (down_rows.reshape(job_slots, ranks, -1) * job_weights[:, None, None]).astype(
        jnp.bfloat16
    )
    up_rows = lax.dot_general(
        act_spread, grad_output, contract_rows, preferred_element_type=jnp.float32
    )
    up_rows = (up_rows.reshape(job_slots, ranks, -1) * job_weights[:, None, None]).astype(
        jnp.bfloat16
    )
    returned_down, returned_up = (
        lax.all_to_all(
            down_rows.reshape(job_slots, ranks, shard_count, down_slab),
            SEQ,
            split_axis=2,
            concat_axis=1,
            tiled=True,
        ),
        lax.all_to_all(
            up_rows.reshape(job_slots, ranks, shard_count, up_slab),
            SEQ,
            split_axis=2,
            concat_axis=1,
            tiled=True,
        ),
    )
    tenant_map = (
        tenant_table.transpose(1, 0, 2)
        .reshape(job_slots * shard_count, tenant_total)
        .astype(jnp.bfloat16)
    )
    grad_adapter_down = lax.dot_general(
        tenant_map,
        returned_down.reshape(job_slots * shard_count, ranks * down_slab),
        contract_rows,
        preferred_element_type=jnp.float32,
    ).reshape(tenant_total, ranks, down_slab)
    grad_adapter_up = lax.dot_general(
        tenant_map,
        returned_up.reshape(job_slots * shard_count, ranks * up_slab),
        contract_rows,
        preferred_element_type=jnp.float32,
    ).reshape(tenant_total, ranks, up_slab)
    return (grad_hidden, grad_adapter_down, grad_adapter_up)


SEQ = ("chip", "core")


def solution(mesh):
    chips = mesh.devices.reshape(mesh.shape["grp"], mesh.shape["seq"] // 2, 2)
    mesh = jax.sharding.Mesh(chips, ("grp", "chip", "core"))
    placed = (
        P(SEQ, "grp"),
        P(SEQ, "grp"),
        P(SEQ, "grp"),
        P(None, None, ("grp", "chip", "core")),
        P(None, None, ("grp", "chip", "core")),
        P(),
        P(),
    )
    return jax.shard_map(
        shards,
        mesh=mesh,
        in_specs=placed,
        out_specs=(
            P(SEQ, "grp"),
            P(None, None, ("grp", "chip", "core")),
            P(None, None, ("grp", "chip", "core")),
        ),
        check_vma=False,
    )
```

profile of v0, /device:TPU:32, one launch (start us, length us, event | category | flops | bytes accessed | tf_op | source)
XLA Modules:
  0.0 504.4 jit_solution(12234305566538353482)
XLA Ops:
  8.7 24.1 %all-gather.5.cloned.1.call-done = bf16[1792,2048]{1,0:T(8,128)(2,1)} async-done(((bf16[896,2048]{1,0:T(8,128)(2,1)}), bf16[1792,2048]{1,0:T(8,128)(2,1)}) %all-gather.5.cloned.1.call-update) | async-done | bytes 7340048 | tf_op jit(solution)/shard_map/all_gather | solution.py:55
  32.8 74.1 %all-gather.3.cloned.1.call-done = bf16[2048,2048]{1,0:T(8,128)(2,1)} async-done(((bf16[128,2048]{1,0:T(8,128)(2,1)}), bf16[2048,2048]{1,0:T(8,128)(2,1)}) %all-gather.3.cloned.1.call-update) | async-done | bytes 8388624 | tf_op jit(solution)/shard_map/all_gather | solution.py:56
  106.9 21.3 %convolution_convert_fusion = bf16[2048,1792]{1,0:T(8,128)(2,1)} fusion(bf16[2048,2048]{1,0:T(8,128)(2,1)} %all-gather.3.cloned.1.call-done, bf16[1792,2048]{1,0:T(8,128)(2,1)} %all-gather.5.cloned.1.call-done), kind=kOutput, calls=%fused_computation.7 | convolution fusion | flops 15036055552 | bytes 23068672 | tf_op jit(solution)/shard_map/dot_general | solution.py:57
  128.2 10.0 %copy.60 = bf16[16,128,1792]{1,2,0:T(8,128)(2,1)} copy(bf16[16,128,1792]{2,1,0:T(8,128)(2,1)} %bitcast.111) | data formatting | bytes 14680064 | tf_op jit(solution)/shard_map/all_to_all | solution.py:60
  138.1 89.2 %all_to_all.76 = bf16[16,128,1792]{1,2,0:T(8,128)(2,1)} all-to-all(bf16[16,128,1792]{1,2,0:T(8,128)(2,1)} %copy.60), channel_id=1, replica_groups=mesh['grp'=4,'chip'=16,'core'=2] {'chip'}, dimensions={0} | all-to-all | bytes 14680064 | tf_op jit(solution)/shard_map/all_to_all | solution.py:60
  227.4 10.0 %copy.61 = bf16[128,4,7168]{2,0,1:T(8,128)(2,1)} copy(bf16[128,4,7168]{0,2,1:T(8,128)(2,1)} %bitcast.104) | data formatting | bytes 14680064 | tf_op jit(solution)/shard_map/reshape | solution.py:65
  240.7 3.2 copy.79
  243.9 4.8 reshape.160
  248.7 5.9 %all-to-all-start.1 = ((bf16[32,2,8192]{2,1,0:T(2,128)(2,1)}), bf16[32,2,8192]{2,1,0:T(2,128)(2,1)S(1)}, u32[]{:S(2)}, u32[]{:S(2)}) async-start(bf16[32,2,8192]{2,1,0:T(2,128)(2,1)} %reshape.160), calls=%async_computation.2 | async-start | bytes 2097152 | tf_op jit(solution)/shard_map/all_to_all | solution.py:38
  254.6 2.8 gather_fusion.1
  257.4 4.8 copy.65
  262.2 7.9 %all-to-all-done.1 = bf16[32,2,8192]{2,1,0:T(2,128)(2,1)S(1)} async-done(((bf16[32,2,8192]{2,1,0:T(2,128)(2,1)}), bf16[32,2,8192]{2,1,0:T(2,128)(2,1)S(1)}, u32[]{:S(2)}, u32[]{:S(2)}) %all-to-all-start.1) | async-done | bytes 1048608 | tf_op jit(solution)/shard_map/all_to_all | solution.py:38
  270.1 6.6 %all-to-all-start.2 = ((bf16[4,32,64,224]{3,2,0,1:T(8,128)(2,1)}), bf16[4,32,64,224]{3,2,0,1:T(8,128)(2,1)}, u32[]{:S(2)}, u32[]{:S(2)}) async-start(bf16[4,32,64,224]{3,2,0,1:T(8,128)(2,1)} %copy.65), calls=%async_computation.3 | async-start | bytes 8388608 | tf_op jit(solution)/shard_map/all_to_all | solution.py:37
  284.5 46.2 %all-to-all-done.2 = bf16[4,32,64,224]{3,2,0,1:T(8,128)(2,1)} async-done(((bf16[4,32,64,224]{3,2,0,1:T(8,128)(2,1)}), bf16[4,32,64,224]{3,2,0,1:T(8,128)(2,1)}, u32[]{:S(2)}, u32[]{:S(2)}) %all-to-all-start.2) | async-done | bytes 3670048 | tf_op jit(solution)/shard_map/all_to_all | solution.py:37
  330.8 6.6 %copy.66 = bf16[4,1,64,32,224]{4,3,2,0,1:T(8,128)(2,1)} copy(bf16[4,1,64,32,224]{4,2,0,3,1:T(8,128)(2,1)} %bitcast.16) | data formatting | bytes 7340032 | tf_op jit(solution)/shard_map/all_to_all | solution.py:37
  337.4 9.0 %reshape.130 = bf16[256,7168]{1,0:T(8,128)(2,1)} reshape(bf16[4,1,64,32,224]{4,3,2,0,1:T(8,128)(2,1)} %copy.66) | data formatting | bytes 7340032 | tf_op jit(solution)/shard_map/reshape | solution.py:40
  346.3 3.1 fusion.23
  349.5 17.6 %psum.7 = bf16[128,128]{0,1:T(8,128)(2,1)S(1)} all-reduce(f32[128,128]{0,1:T(8,128)S(1)} %maximum_convert_fusion), channel_id=1, replica_groups=mesh['grp'=4,'chip'=16,'core'=2] {'grp'}, use_global_device_ids=true, to_apply=%region_4.5 | all-reduce | flops 16384 | bytes 98304 | tf_op jit(solution)/shard_map/psum | solution.py:67
  368.6 3.3 reshape.134
  374.1 4.8 reshape.162
  378.9 5.2 %all-to-all-start.4 = ((bf16[32,2,8192]{2,1,0:T(2,128)(2,1)}), bf16[32,2,8192]{2,1,0:T(2,128)(2,1)S(1)}, u32[]{:S(2)}, u32[]{:S(2)}) async-start(bf16[32,2,8192]{2,1,0:T(2,128)(2,1)} %reshape.162), calls=%async_computation.5 | async-start | bytes 2097152 | tf_op jit(solution)/shard_map/all_to_all | solution.py:104
  384.1 3.0 fusion
  387.1 8.8 %reshape.132 = bf16[4,64,32,224]{3,2,1,0:T(8,128)(2,1)} reshape(bf16[4,64,7168]{2,1,0:T(8,128)(2,1)} %fusion) | data formatting | bytes 7340032 | tf_op jit(solution)/shard_map/reshape | solution.py:98
  395.9 6.6 %copy.67 = bf16[4,64,32,224]{3,1,0,2:T(8,128)(2,1)} copy(bf16[4,64,32,224]{3,2,1,0:T(8,128)(2,1)} %reshape.132) | data formatting | bytes 7340032 | tf_op jit(solution)/shard_map/reshape | solution.py:98
  402.5 7.8 %all-to-all-start.3 = ((bf16[4,64,32,224]{3,1,0,2:T(8,128)(2,1)}), bf16[4,64,32,224]{3,1,0,2:T(8,128)(2,1)}, u32[]{:S(2)}, u32[]{:S(2)}) async-start(bf16[4,64,32,224]{3,1,0,2:T(8,128)(2,1)} %copy.67), calls=%async_computation.4 | async-start | bytes 8388608 | tf_op jit(solution)/shard_map/all_to_all | solution.py:97
  420.1 44.4 %all-to-all-done.3 = bf16[4,64,32,224]{3,1,0,2:T(8,128)(2,1)} async-done(((bf16[4,64,32,224]{3,1,0,2:T(8,128)(2,1)}), bf16[4,64,32,224]{3,1,0,2:T(8,128)(2,1)}, u32[]{:S(2)}, u32[]{:S(2)}) %all-to-all-start.3) | async-done | bytes 3670048 | tf_op jit(solution)/shard_map/all_to_all | solution.py:97
  464.4 4.8 copy.68
  469.2 8.5 %reshape.133 = bf16[128,14336]{1,0:T(8,128)(2,1)} reshape(bf16[4,32,64,1,224]{4,2,1,0,3:T(8,128)(2,1)} %copy.68) | data formatting | bytes 7340032 | tf_op jit(solution)/shard_map/reshape | solution.py:119
  477.8 6.0 %copy.69 = bf16[14336,128]{1,0:T(8,128)(2,1)} copy(bf16[14336,128]{0,1:T(8,128)(2,1)} %bitcast.107) | data formatting | bytes 7340032 | tf_op jit(solution)/shard_map/dot_general | solution.py:117
  483.8 4.4 fusion.14
  488.2 4.4 copy.73
  492.7 5.0 fusion.2
  (60 shorter events, 25.8 us)
Async XLA Ops:
  7.2 247.4 %copy-start = (bf16[64,64,224]{2,1,0:T(8,128)(2,1)S(1)}, bf16[64,64,224]{2,1,0:T(8,128)(2,1)}, u32[]{:S(2)}) copy-start(bf16[64,64,224]{2,1,0:T(8,128)(2,1)} %param.10) | copy-start | bytes 5505028
  7.2 25.6 %all-gather.5.cloned.1.call-start = ((), (), s32[]{:S(2)}) async-start(), calls=%async_computation.7 | async-start | bytes 11010048 | tf_op jit(solution)/shard_map/all_gather | solution.py:55
  7.9 99.0 %all-gather.3.cloned.1.call-start = ((), (), s32[]{:S(2)}) async-start(), calls=%async_computation.6 | async-start | bytes 8912896 | tf_op jit(solution)/shard_map/all_gather | solution.py:56
  8.7 484.0 %reduce-scatter.2.cloned.1.call-start = ((), (), s32[]{:S(2)}) async-start(), calls=%async_computation.8 | async-start | bytes 9175040 | tf_op jit(solution)/shard_map/reduce_scatter | solution.py:64
  237.3 0.7 copy-start.6
  237.3 1.2 copy-start.5
  248.7 21.5 %all-to-all-start.1 = ((bf16[32,2,8192]{2,1,0:T(2,128)(2,1)}), bf16[32,2,8192]{2,1,0:T(2,128)(2,1)S(1)}, u32[]{:S(2)}, u32[]{:S(2)}) async-start(bf16[32,2,8192]{2,1,0:T(2,128)(2,1)} %reshape.160), calls=%async_computation.2 | async-start | bytes 2097152 | tf_op jit(solution)/shard_map/all_to_all | solution.py:38
  262.2 14.5 %copy-start.7 = (s32[32,4]{0,1:T(4,128)S(1)}, s32[32,4]{0,1:T(4,128)}, u32[]{:S(2)}) copy-start(s32[32,4]{0,1:T(4,128)} %param.13) | copy-start | bytes 1540
  270.1 60.6 %all-to-all-start.2 = ((bf16[4,32,64,224]{3,2,0,1:T(8,128)(2,1)}), bf16[4,32,64,224]{3,2,0,1:T(8,128)(2,1)}, u32[]{:S(2)}, u32[]{:S(2)}) async-start(bf16[4,32,64,224]{3,2,0,1:T(8,128)(2,1)} %copy.65), calls=%async_computation.3 | async-start | bytes 8388608 | tf_op jit(solution)/shard_map/all_to_all | solution.py:37
  279.1 3.8 copy-start.4
  337.4 9.0 %copy-start.2 = (bf16[128,7168]{1,0:T(8,128)(2,1)S(1)}, bf16[128,7168]{1,0:T(8,128)(2,1)}, u32[]{:S(2)}) copy-start(bf16[128,7168]{1,0:T(8,128)(2,1)} %param.8) | copy-start | bytes 5505028
  374.1 10.0 %copy-start.3 = (bf16[128,7168]{1,0:T(8,128)(2,1)S(1)}, bf16[128,7168]{1,0:T(8,128)(2,1)}, u32[]{:S(2)}) copy-start(bf16[128,7168]{1,0:T(8,128)(2,1)} %param.8) | copy-start | bytes 5505028
  378.9 23.7 %all-to-all-start.4 = ((bf16[32,2,8192]{2,1,0:T(2,128)(2,1)}), bf16[32,2,8192]{2,1,0:T(2,128)(2,1)S(1)}, u32[]{:S(2)}, u32[]{:S(2)}) async-start(bf16[32,2,8192]{2,1,0:T(2,128)(2,1)} %reshape.162), calls=%async_computation.5 | async-start | bytes 2097152 | tf_op jit(solution)/shard_map/all_to_all | solution.py:104
  402.5 61.9 %all-to-all-start.3 = ((bf16[4,64,32,224]{3,1,0,2:T(8,128)(2,1)}), bf16[4,64,32,224]{3,1,0,2:T(8,128)(2,1)}, u32[]{:S(2)}, u32[]{:S(2)}) async-start(bf16[4,64,32,224]{3,1,0,2:T(8,128)(2,1)} %copy.67), calls=%async_computation.4 | async-start | bytes 8388608 | tf_op jit(solution)/shard_map/all_to_all | solution.py:97
  492.7 5.0 copy-start.1
Sparse Core Ops, SparseCore 0:
  9.7 23.0 all-gather.4
  34.9 71.9 all-gather.2
  237.5 72.3 reduce-scatter.1
where the time goes:
time: 513 us; the launch traced here: 504 us
  waiting for transfers between devices  198 us (39%)
  local copies, waits for them, and re-layouts  117 us (23%)
  blocking collectives  107 us (21%)
  matrix products  42.2 us (8%)
  starting transfers between devices  25.6 us (5%)
  between operations  14.2 us (3%)
    all_to_all x1, blocking collectives, shards(): lax.all_to_all(partial_value.astype(jnp.bfloat16), 'chip', split_axis=0,...  89.2 us
    all_gather x1, waiting for transfers between devices, shards(): tokens_same_core = lax.all_gather(grad_output, 'chip', axis=0, tiled=True)  74.1 us
    all_to_all x1, waiting for transfers between devices, shards(): lax.all_to_all(adapter_down[chosen], SEQ, split_axis=1, concat_axis=3, ti...  46.2 us
    all_to_all x1, waiting for transfers between devices, shards(): lax.all_to_all(down_rows.reshape(job_slots, ranks, shard_count, down_slab...  44.4 us
    all_gather x1, waiting for transfers between devices, shards(): weight_pair = lax.all_gather(down_weight, 'core', axis=0, tiled=True)  24.1 us
    dot_general x1, matrix products, shards(): lax.dot_general(tokens_same_core, weight_pair, contract_last, preferred_e...  21.3 us
    unnamed x23, local copies, waits for them, and re-layouts  20.5 us
    psum x1, blocking collectives, shards(): rank_sum = lax.psum(rank_part.astype(jnp.float32), 'grp')  17.6 us
  transfers between devices with their start and end apart: 7, of which 5 were waited for; matrix products, arithmetic and copies ran while one was open for 22% of the time, Pallas kernels for 0%

commit v1 on v0

--- a/solution.py
+++ b/solution.py
@@ -2,6 +2,7 @@
 import jax.numpy as jnp
 from jax import lax
 from jax.sharding import PartitionSpec as P
+from jax.lax import all_to_all, psum
 
 ADAPTER_SCALE = 2.0
 
@@ -52,7 +53,15 @@
     rank_part = jnp.concatenate([select_jobs(grad_proj), select_jobs(act_proj)], axis=1).astype(
         jnp.bfloat16
     )
-    weight_pair = lax.all_gather(down_weight, "core", axis=0, tiled=True)
+    weight_pair = jnp.concatenate(
+        all_to_all(
+            jnp.stack([down_weight for _ in range(psum(1, "core"))]),
+            axis_name="core",
+            split_axis=0,
+            concat_axis=0,
+        ),
+        axis=0,
+    )
     tokens_same_core = lax.all_gather(grad_output, "chip", axis=0, tiled=True)
     partial_value = lax.dot_general(
         tokens_same_core, weight_pair, contract_last, preferred_element_type=jnp.float32

time: 513 us -> 485 us (0.945)
  waiting for transfers between devices: 198 us -> 159 us
  blocking collectives: 107 us -> 118 us
    all_gather x1 -> x0, waiting for transfers between devices: 24.1 us -> none  [shards(): weight_pair = lax.all_gather(down_weight, 'core', axis=0, tiled=True)]
    all_gather x1, waiting for transfers between devices: 74.1 us -> 60.2 us  [shards(): tokens_same_core = lax.all_gather(grad_output, 'chip', axis=0, tiled=True)]
    all_to_all x0 -> x1, blocking collectives: none -> 10.9 us  [shards(): all_to_all(jnp.stack([down_weight for _ in range(psum(1, 'core'))]), axis...]
  transfers between devices with their start and end apart: 7 -> 6, of which waited for: 5 -> 4; matrix products, arithmetic and copies ran while one was open for 22% -> 24% of each run, Pallas kernels for 0% -> 0%
where the time goes in v1:
time: 485 us; the launch traced here: 476 us
  waiting for transfers between devices  159 us (33%)
  blocking collectives  118 us (24%)
  local copies, waits for them, and re-layouts  112 us (23%)
  matrix products  42.3 us (9%)
  starting transfers between devices  25.6 us (5%)
  between operations  14.5 us (3%)
    all_to_all x1, blocking collectives, shards(): lax.all_to_all(partial_value.astype(jnp.bfloat16), 'chip', split_axis=0,...  89 us
    all_gather x1, waiting for transfers between devices, shards(): tokens_same_core = lax.all_gather(grad_output, 'chip', axis=0, tiled=True)  60.2 us
    all_to_all x1, waiting for transfers between devices, shards(): lax.all_to_all(adapter_down[chosen], SEQ, split_axis=1, concat_axis=3, ti...  46.2 us
    all_to_all x1, waiting for transfers between devices, shards(): lax.all_to_all(down_rows.reshape(job_slots, ranks, shard_count, down_slab...  44.4 us
    dot_general x1, matrix products, shards(): lax.dot_general(tokens_same_core, weight_pair, contract_last, preferred_e...  21.4 us
    unnamed x23, local copies, waits for them, and re-layouts  20.5 us
    psum x1, blocking collectives, shards(): rank_sum = lax.psum(rank_part.astype(jnp.float32), 'grp')  17.6 us
    reshape x2, local copies, waits for them, and re-layouts, shards(): down_rows.reshape(job_slots, ranks, shard_count, down_slab)  15.4 us
  transfers between devices with their start and end apart: 6, of which 4 were waited for; matrix products, arithmetic and copies ran while one was open for 24% of the time, Pallas kernels for 0%

profile of v1, /device:TPU:32, one launch (start us, length us, event | category | flops | bytes accessed | tf_op | source)
XLA Modules:
  0.0 475.7 jit_solution(15583050622166900107)
XLA Ops:
  8.0 3.8 pad_maximum_fusion
  11.8 10.9 %all_to_all.81 = bf16[2,896,2048]{2,1,0:T(8,128)(2,1)} all-to-all(bf16[2,896,2048]{2,1,0:T(8,128)(2,1)S(1)} %pad_maximum_fusion), channel_id=1, replica_groups=mesh['grp'=4,'chip'=16,'core'=2] {'core'}, dimensions={0} | all-to-all | bytes 14680064 | tf_op jit(solution)/shard_map/all_to_all | solution.py:57
  22.7 60.2 %all-gather.2.cloned.1.call-done = bf16[2048,2048]{1,0:T(8,128)(2,1)} async-done(((bf16[128,2048]{1,0:T(8,128)(2,1)}), bf16[2048,2048]{1,0:T(8,128)(2,1)}) %all-gather.2.cloned.1.call-update) | async-done | bytes 8388624 | tf_op jit(solution)/shard_map/all_gather | solution.py:65
  82.9 21.4 %fusion.3 = bf16[224,16,8,128]{3,2,1,0:T(8,128)(2,1)} fusion(bf16[1792,2048]{1,0:T(8,128)(2,1)} %bitcast.119, bf16[2048,2048]{1,0:T(8,128)(2,1)} %all-gather.2.cloned.1.call-done), kind=kOutput, calls=%fused_computation.10 | convolution fusion | flops 15036055552 | bytes 23068672 | tf_op jit(solution)/shard_map/dot_general | solution.py:66
  104.3 5.0 %copy.80 = bf16[224,16,8,128]{3,2,0,1:T(8,128)(2,1)S(1)} copy(bf16[224,16,8,128]{3,2,1,0:T(8,128)(2,1)} %fusion.3) | data formatting | bytes 14680064 | tf_op jit(solution)/shard_map/all_to_all | solution.py:69
  109.3 89.0 %all_to_all.82 = bf16[16,128,1792]{1,2,0:T(8,128)(2,1)} all-to-all(bf16[16,128,1792]{1,2,0:T(8,128)(2,1)S(1)} %bitcast.111), channel_id=1, replica_groups=mesh['grp'=4,'chip'=16,'core'=2] {'chip'}, dimensions={0} | all-to-all | bytes 14680064 | tf_op jit(solution)/shard_map/all_to_all | solution.py:69
  198.3 10.0 %copy.61 = bf16[128,4,7168]{2,0,1:T(8,128)(2,1)} copy(bf16[128,4,7168]{0,2,1:T(8,128)(2,1)} %bitcast.112) | data formatting | bytes 14680064 | tf_op jit(solution)/shard_map/reshape | solution.py:74
  211.7 3.2 copy.82
  214.8 4.8 %reshape.164 = bf16[32,2,8192]{2,1,0:T(2,128)(2,1)} reshape(bf16[32,4,64,64]{3,2,1,0:T(8,128)(2,1)} %bitcast.116) | data formatting | bytes 2097152
  219.7 5.9 %all-to-all-start.2 = ((bf16[32,2,8192]{2,1,0:T(2,128)(2,1)}), bf16[32,2,8192]{2,1,0:T(2,128)(2,1)S(1)}, u32[]{:S(2)}, u32[]{:S(2)}) async-start(bf16[32,2,8192]{2,1,0:T(2,128)(2,1)} %reshape.164), calls=%async_computation.3 | async-start | bytes 2097152 | tf_op jit(solution)/shard_map/all_to_all | solution.py:39
  228.4 4.8 %copy.65 = bf16[4,32,64,224]{3,2,0,1:T(8,128)(2,1)} copy(bf16[4,32,64,224]{3,2,1,0:T(8,128)(2,1)} %bitcast.113) | data formatting | bytes 7340032 | tf_op jit(solution)/shard_map/gather | solution.py:38
  233.2 7.9 %all-to-all-done.2 = bf16[32,2,8192]{2,1,0:T(2,128)(2,1)S(1)} async-done(((bf16[32,2,8192]{2,1,0:T(2,128)(2,1)}), bf16[32,2,8192]{2,1,0:T(2,128)(2,1)S(1)}, u32[]{:S(2)}, u32[]{:S(2)}) %all-to-all-start.2) | async-done | bytes 1048608 | tf_op jit(solution)/shard_map/all_to_all | solution.py:39
  241.1 6.6 %all-to-all-start.3 = ((bf16[4,32,64,224]{3,2,0,1:T(8,128)(2,1)}), bf16[4,32,64,224]{3,2,0,1:T(8,128)(2,1)}, u32[]{:S(2)}, u32[]{:S(2)}) async-start(bf16[4,32,64,224]{3,2,0,1:T(8,128)(2,1)} %copy.65), calls=%async_computation.4 | async-start | bytes 8388608 | tf_op jit(solution)/shard_map/all_to_all | solution.py:38
  255.5 46.2 %all-to-all-done.3 = bf16[4,32,64,224]{3,2,0,1:T(8,128)(2,1)} async-done(((bf16[4,32,64,224]{3,2,0,1:T(8,128)(2,1)}), bf16[4,32,64,224]{3,2,0,1:T(8,128)(2,1)}, u32[]{:S(2)}, u32[]{:S(2)}) %all-to-all-start.3) | async-done | bytes 3670048 | tf_op jit(solution)/shard_map/all_to_all | solution.py:38
  301.8 6.6 %copy.66 = bf16[4,1,64,32,224]{4,3,2,0,1:T(8,128)(2,1)} copy(bf16[4,1,64,32,224]{4,2,0,3,1:T(8,128)(2,1)} %bitcast.18) | data formatting | bytes 7340032 | tf_op jit(solution)/shard_map/all_to_all | solution.py:38
  308.4 8.9 %reshape.134 = bf16[256,7168]{1,0:T(8,128)(2,1)} reshape(bf16[4,1,64,32,224]{4,3,2,0,1:T(8,128)(2,1)} %copy.66) | data formatting | bytes 7340032 | tf_op jit(solution)/shard_map/reshape | solution.py:41
  317.3 3.1 fusion.24
  320.5 17.6 %psum.7 = bf16[128,128]{0,1:T(8,128)(2,1)S(1)} all-reduce(f32[128,128]{0,1:T(8,128)S(1)} %maximum_convert_fusion), channel_id=1, replica_groups=mesh['grp'=4,'chip'=16,'core'=2] {'grp'}, use_global_device_ids=true, to_apply=%region_4.5 | all-reduce | flops 16384 | bytes 98304 | tf_op jit(solution)/shard_map/psum | solution.py:76
  339.6 3.3 reshape.138
  345.0 4.8 %reshape.166 = bf16[32,2,8192]{2,1,0:T(2,128)(2,1)} reshape(bf16[32,4,64,64]{3,2,1,0:T(8,128)(2,1)} %bitcast.117) | data formatting | bytes 2097152
  349.8 5.2 %all-to-all-start.5 = ((bf16[32,2,8192]{2,1,0:T(2,128)(2,1)}), bf16[32,2,8192]{2,1,0:T(2,128)(2,1)S(1)}, u32[]{:S(2)}, u32[]{:S(2)}) async-start(bf16[32,2,8192]{2,1,0:T(2,128)(2,1)} %reshape.166), calls=%async_computation.6 | async-start | bytes 2097152 | tf_op jit(solution)/shard_map/all_to_all | solution.py:113
  355.0 3.0 fusion
  358.0 8.8 %reshape.136 = bf16[4,64,32,224]{3,2,1,0:T(8,128)(2,1)} reshape(bf16[4,64,7168]{2,1,0:T(8,128)(2,1)} %fusion) | data formatting | bytes 7340032 | tf_op jit(solution)/shard_map/reshape | solution.py:107
  366.9 6.6 %copy.67 = bf16[4,64,32,224]{3,1,0,2:T(8,128)(2,1)} copy(bf16[4,64,32,224]{3,2,1,0:T(8,128)(2,1)} %reshape.136) | data formatting | bytes 7340032 | tf_op jit(solution)/shard_map/reshape | solution.py:107
  373.5 7.8 %all-to-all-start.4 = ((bf16[4,64,32,224]{3,1,0,2:T(8,128)(2,1)}), bf16[4,64,32,224]{3,1,0,2:T(8,128)(2,1)}, u32[]{:S(2)}, u32[]{:S(2)}) async-start(bf16[4,64,32,224]{3,1,0,2:T(8,128)(2,1)} %copy.67), calls=%async_computation.5 | async-start | bytes 8388608 | tf_op jit(solution)/shard_map/all_to_all | solution.py:106
  391.0 44.4 %all-to-all-done.4 = bf16[4,64,32,224]{3,1,0,2:T(8,128)(2,1)} async-done(((bf16[4,64,32,224]{3,1,0,2:T(8,128)(2,1)}), bf16[4,64,32,224]{3,1,0,2:T(8,128)(2,1)}, u32[]{:S(2)}, u32[]{:S(2)}) %all-to-all-start.4) | async-done | bytes 3670048 | tf_op jit(solution)/shard_map/all_to_all | solution.py:106
  435.4 4.8 %copy.68 = bf16[4,32,64,1,224]{4,2,1,0,3:T(8,128)(2,1)} copy(bf16[4,32,64,1,224]{4,2,0,1,3:T(8,128)(2,1)} %bitcast.28) | data formatting | bytes 7340032 | tf_op jit(solution)/shard_map/all_to_all | solution.py:106
  440.2 8.5 %reshape.137 = bf16[128,14336]{1,0:T(8,128)(2,1)} reshape(bf16[4,32,64,1,224]{4,2,1,0,3:T(8,128)(2,1)} %copy.68) | data formatting | bytes 7340032 | tf_op jit(solution)/shard_map/reshape | solution.py:128
  448.7 6.0 %copy.69 = bf16[14336,128]{1,0:T(8,128)(2,1)} copy(bf16[14336,128]{0,1:T(8,128)(2,1)} %bitcast.115) | data formatting | bytes 7340032 | tf_op jit(solution)/shard_map/dot_general | solution.py:126
  454.7 4.4 fusion.15
  459.1 4.5 copy.73
  463.6 5.0 %fusion.2 = bf16[128,7168]{1,0:T(8,128)(2,1)} fusion(bf16[128,256]{0,1:T(8,128)(2,1)S(1)} %bitcast.125, bf16[256,7168]{1,0:T(8,128)(2,1)} %reshape.134, bf16[128,1,7168]{2,0,1:T(8,128)(2,1)} %reduce-scatter.2.cloned.1.call-done), kind=kOutput, calls=%fused_computation.6 | convolution fusion | flops 473432064 | bytes 7405568 | tf_op jit(solution)/shard_map/dot_general | solution.py:90
  (59 shorter events, 27.9 us)
Async XLA Ops:
  7.2 218.4 %copy-start = (bf16[64,64,224]{2,1,0:T(8,128)(2,1)S(1)}, bf16[64,64,224]{2,1,0:T(8,128)(2,1)}, u32[]{:S(2)}) copy-start(bf16[64,64,224]{2,1,0:T(8,128)(2,1)} %param.10) | copy-start | bytes 5505028
  7.2 75.7 %all-gather.2.cloned.1.call-start = ((), (), s32[]{:S(2)}) async-start(), calls=%async_computation.7 | async-start | bytes 8912896 | tf_op jit(solution)/shard_map/all_gather | solution.py:65
  7.9 455.7 %reduce-scatter.2.cloned.1.call-start = ((), (), s32[]{:S(2)}) async-start(), calls=%async_computation.8 | async-start | bytes 9175040 | tf_op jit(solution)/shard_map/reduce_scatter | solution.py:73
  208.3 0.7 copy-start.6
  208.3 1.2 copy-start.5
  219.7 21.5 %all-to-all-start.2 = ((bf16[32,2,8192]{2,1,0:T(2,128)(2,1)}), bf16[32,2,8192]{2,1,0:T(2,128)(2,1)S(1)}, u32[]{:S(2)}, u32[]{:S(2)}) async-start(bf16[32,2,8192]{2,1,0:T(2,128)(2,1)} %reshape.164), calls=%async_computation.3 | async-start | bytes 2097152 | tf_op jit(solution)/shard_map/all_to_all | solution.py:39
  233.2 14.5 %copy-start.7 = (s32[32,4]{0,1:T(4,128)S(1)}, s32[32,4]{0,1:T(4,128)}, u32[]{:S(2)}) copy-start(s32[32,4]{0,1:T(4,128)} %param.13) | copy-start | bytes 1540
  241.1 60.6 %all-to-all-start.3 = ((bf16[4,32,64,224]{3,2,0,1:T(8,128)(2,1)}), bf16[4,32,64,224]{3,2,0,1:T(8,128)(2,1)}, u32[]{:S(2)}, u32[]{:S(2)}) async-start(bf16[4,32,64,224]{3,2,0,1:T(8,128)(2,1)} %copy.65), calls=%async_computation.4 | async-start | bytes 8388608 | tf_op jit(solution)/shard_map/all_to_all | solution.py:38
  250.1 3.8 copy-start.4
  308.4 8.9 %copy-start.2 = (bf16[128,7168]{1,0:T(8,128)(2,1)S(1)}, bf16[128,7168]{1,0:T(8,128)(2,1)}, u32[]{:S(2)}) copy-start(bf16[128,7168]{1,0:T(8,128)(2,1)} %param.8) | copy-start | bytes 5505028
  345.0 10.0 %copy-start.3 = (bf16[128,7168]{1,0:T(8,128)(2,1)S(1)}, bf16[128,7168]{1,0:T(8,128)(2,1)}, u32[]{:S(2)}) copy-start(bf16[128,7168]{1,0:T(8,128)(2,1)} %param.8) | copy-start | bytes 5505028
  349.8 23.7 %all-to-all-start.5 = ((bf16[32,2,8192]{2,1,0:T(2,128)(2,1)}), bf16[32,2,8192]{2,1,0:T(2,128)(2,1)S(1)}, u32[]{:S(2)}, u32[]{:S(2)}) async-start(bf16[32,2,8192]{2,1,0:T(2,128)(2,1)} %reshape.166), calls=%async_computation.6 | async-start | bytes 2097152 | tf_op jit(solution)/shard_map/all_to_all | solution.py:113
  373.5 61.9 %all-to-all-start.4 = ((bf16[4,64,32,224]{3,1,0,2:T(8,128)(2,1)}), bf16[4,64,32,224]{3,1,0,2:T(8,128)(2,1)}, u32[]{:S(2)}, u32[]{:S(2)}) async-start(bf16[4,64,32,224]{3,1,0,2:T(8,128)(2,1)} %copy.67), calls=%async_computation.5 | async-start | bytes 8388608 | tf_op jit(solution)/shard_map/all_to_all | solution.py:106
  463.6 5.0 %copy-start.1 = (bf16[64,64,224]{2,1,0:T(8,128)(2,1)S(1)}, bf16[64,64,224]{2,1,0:T(8,128)(2,1)}, u32[]{:S(2)}) copy-start(bf16[64,64,224]{2,1,0:T(8,128)(2,1)} %param.10) | copy-start | bytes 5505028
Sparse Core Ops, SparseCore 0:
  10.2 72.6 all-gather.1
  208.5 72.2 reduce-scatter.1
